TPU v7x, 32 devices: a whole 2x2x4 slice. The times are simulated.
32 devices in a mesh: rows: 16 (over z, y, core), cent: 2 (over x).
Axes of the slice: x: 2, y: 2, z: 4, core: 2. Of those that a mesh axis runs over, the one named last changes fastest.
Arguments:
- vectors: bfloat16 [32768, 1024], P('rows'), may hold values from -40 to 40
- centroids: bfloat16 [1024, 4096], P('rows', 'cent'), may hold values from -8 to 8
Outputs:
- centroid_sums: float32 [1024, 4096], P('rows', 'cent')
All inputs are finite; a program needn't handle non-finite values.
Results may differ from a plain program's by a relative error of at most 0.0017.
Values may be sent and summed in bfloat16 or wider, within the bound.
A program may use at most 64 MiB of HBM per device.

v0:
```python
import math
import jax
import jax.numpy as jnp
from jax import lax
from jax.sharding import PartitionSpec as P

K = 4096
ITERS = 3
sharpness = 3.0


def on_device(vectors, centroids):
    row_count = vectors.shape[0]
    width = vectors.shape[1]
    window = vectors
    scores = jnp.dot(
        window,
        lax.all_gather(centroids, "rows", axis=0, tiled=True),
        preferred_element_type=jnp.float32,
    )
    scores = scores * (sharpness / math.sqrt(width))
    row_top = lax.pmax(jnp.max(scores, axis=1), "cent")
    numerator = jnp.exp(scores - row_top[:, None])
    row_total = lax.psum(jnp.sum(numerator, axis=1), "cent")
    balanced = numerator / row_total[:, None]
    target = row_count * lax.axis_size("rows") / K
    for iteration in range(ITERS):
        column_sum = jnp.sum(balanced, axis=0)
        column_mass = lax.psum(column_sum, "rows")
        column_scale = target / column_mass
        balanced = balanced * column_scale[None, :]
        row_mass = lax.psum(jnp.sum(balanced, axis=1), "cent")
        balanced = balanced / row_mass[:, None]
    weights = balanced.astype(jnp.bfloat16)
    factor = K / (row_count * lax.axis_size("rows"))
    window = vectors
    mine = lax.psum_scatter(
        lax.dot_general(
            window, weights, (((0,), (0,)), ((), ())), preferred_element_type=jnp.float32
        ),
        "rows",
        scatter_dimension=0,
        tiled=True,
    )
    return mine * factor


def solution(mesh):
    return jax.shard_map(
        on_device,
        mesh=mesh,
        in_specs=(P("rows", None), P("rows", "cent")),
        out_specs=P("rows", "cent"),
        check_vma=False,
    )
```

profile of v0, /device:TPU:0, one launch (start us, length us, event | category | flops | bytes accessed | tf_op | source)
XLA Modules:
  0.0 386.2 jit_solution(11446826470317669100)
XLA Ops:
  6.5 0.0 all-gather.2.cloned.1.call-start
  6.5 0.7 all-gather.2.cloned.1.call-update
  7.3 0.0 reduce-scatter.4.cloned.1.call-start
  7.3 55.3 %all-gather.2.cloned.1.call-done = bf16[1024,2048]{1,0:T(8,128)(2,1)} async-done(((bf16[64,2048]{1,0:T(8,128)(2,1)}), bf16[1024,2048]{1,0:T(8,128)(2,1)}) %all-gather.2.cloned.1.call-update) | async-done | bytes 4194320 | tf_op jit(solution)/shard_map/all_gather | solution.py:18
  62.6 15.2 %multiply_reduce_fusion.3 = (f32[2048]{0:T(1024)S(1)}, f32[2048,2048]{0,1:T(8,128)}) fusion(bf16[2048,1024]{1,0:T(8,128)(2,1)} %param.2, bf16[1024,2048]{1,0:T(8,128)(2,1)} %all-gather.2.cloned.1.call-done), kind=kOutput, calls=%fused_computation.7 | convolution fusion | flops 8598321152 | bytes 25174016 | tf_op jit(solution)/shard_map/dot_general | solution.py:16
  77.9 5.0 %pmax.7 = f32[2048]{0:T(1024)S(1)} all-reduce(f32[2048]{0:T(1024)S(1)} %get-tuple-element.7), channel_id=1, replica_groups=mesh['rows'=16,'cent'=2] {'cent'}, use_global_device_ids=true, to_apply=%region_1.0 | all-reduce | flops 2048 | bytes 16384 | tf_op jit(solution)/shard_map/pmax | solution.py:22
  82.8 8.5 %fusion.1 = f32[2048]{0:T(1024)S(1)} fusion(f32[2048,2048]{0,1:T(8,128)} %get-tuple-element.8, f32[2048]{0:T(1024)S(1)} %pmax.7), kind=kLoop, calls=%fused_computation.9 | loop fusion | flops 12580864 | bytes 16793600 | tf_op jit(solution)/shard_map/reduce_sum | solution.py:24
  91.4 5.0 %psum.49 = f32[2048]{0:T(1024)S(1)} all-reduce(f32[2048]{0:T(1024)S(1)} %fusion.1), channel_id=1, replica_groups=mesh['rows'=16,'cent'=2] {'cent'}, use_global_device_ids=true, to_apply=%region_3.0 | all-reduce | flops 2048 | bytes 16384 | tf_op jit(solution)/shard_map/psum | solution.py:24
  96.4 7.7 %fusion.4 = f32[2048]{0:T(1024)S(1)} fusion(f32[2048]{0:T(1024)S(1)} %psum.49, f32[2048]{0:T(1024)S(1)} %pmax.7, f32[2048,2048]{0,1:T(8,128)} %get-tuple-element.8), kind=kLoop, calls=%fused_computation.16 | loop fusion | flops 16775168 | bytes 16801792 | tf_op jit(solution)/shard_map/reduce_sum | solution.py:28
  104.1 30.0 %psum.50 = f32[2048]{0:T(1024)S(1)} all-reduce(f32[2048]{0:T(1024)S(1)} %fusion.4), channel_id=1, replica_groups=mesh['rows'=16,'cent'=2] {'rows'}, use_global_device_ids=true, to_apply=%region_5.0 | all-reduce | flops 2048 | bytes 16384 | tf_op jit(solution)/shard_map/psum | solution.py:29
  134.1 8.1 %multiply_reduce_fusion.2 = f32[2048]{0:T(1024)S(1)} fusion(f32[2048]{0:T(1024)S(1)} %broadcast_divide_fusion.2, f32[2048]{0:T(1024)S(1)} %psum.49, f32[2048]{0:T(1024)S(1)} %pmax.7, f32[2048,2048]{0,1:T(8,128)} %get-tuple-element.8), kind=kLoop, calls=%fused_computation.6 | loop fusion | flops 20969472 | bytes 16809984 | tf_op jit(solution)/shard_map/reduce_sum | solution.py:32
  142.2 5.0 %psum.51 = f32[2048]{0:T(1024)S(1)} all-reduce(f32[2048]{0:T(1024)S(1)} %multiply_reduce_fusion.2), channel_id=1, replica_groups=mesh['rows'=16,'cent'=2] {'cent'}, use_global_device_ids=true, to_apply=%region_7.0 | all-reduce | flops 2048 | bytes 16384 | tf_op jit(solution)/shard_map/psum | solution.py:32
  147.2 13.1 %fusion.6 = (f32[2048]{0:T(1024)S(1)}, f32[2048,2048]{0,1:T(8,128)}) fusion(f32[2048]{0:T(1024)S(1)} %psum.51, f32[2048]{0:T(1024)S(1)} %broadcast_divide_fusion.2, f32[2048]{0:T(1024)S(1)} %psum.49, f32[2048]{0:T(1024)S(1)} %pmax.7, f32[2048,2048]{0,1:T(8,128)} %get-tuple-element.8), kind=kLoop, calls=%fused_computation.18 | loop fusion | flops 25163776 | bytes 33595392 | tf_op jit(solution)/shard_map/reduce_sum | solution.py:28
  160.3 30.2 %psum.52 = f32[2048]{0:T(1024)S(1)} all-reduce(f32[2048]{0:T(1024)S(1)} %get-tuple-element.5), channel_id=1, replica_groups=mesh['rows'=16,'cent'=2] {'rows'}, use_global_device_ids=true, to_apply=%region_9.0 | all-reduce | flops 2048 | bytes 16384 | tf_op jit(solution)/shard_map/psum | solution.py:29
  190.5 6.9 %multiply_reduce_fusion.1 = f32[2048]{0:T(1024)S(1)} fusion(f32[2048,2048]{0,1:T(8,128)} %get-tuple-element.6, f32[2048]{0:T(1024)S(1)} %broadcast_divide_fusion.1), kind=kLoop, calls=%fused_computation.4 | loop fusion | flops 8386560 | bytes 16793600 | tf_op jit(solution)/shard_map/reduce_sum | solution.py:32
  197.4 5.0 %psum.53 = f32[2048]{0:T(1024)S(1)} all-reduce(f32[2048]{0:T(1024)S(1)} %multiply_reduce_fusion.1), channel_id=1, replica_groups=mesh['rows'=16,'cent'=2] {'cent'}, use_global_device_ids=true, to_apply=%region_11.0 | all-reduce | flops 2048 | bytes 16384 | tf_op jit(solution)/shard_map/psum | solution.py:32
  202.5 7.1 %fusion.5 = f32[2048]{0:T(1024)S(1)} fusion(f32[2048]{0:T(1024)S(1)} %psum.53, f32[2048,2048]{0,1:T(8,128)} %get-tuple-element.6, f32[2048]{0:T(1024)S(1)} %broadcast_divide_fusion.1), kind=kLoop, calls=%fused_computation.17 | loop fusion | flops 12580864 | bytes 16801792 | tf_op jit(solution)/shard_map/reduce_sum | solution.py:28
  209.6 30.0 %psum.54 = f32[2048]{0:T(1024)S(1)} all-reduce(f32[2048]{0:T(1024)S(1)} %fusion.5), channel_id=1, replica_groups=mesh['rows'=16,'cent'=2] {'rows'}, use_global_device_ids=true, to_apply=%region_13.0 | all-reduce | flops 2048 | bytes 16384 | tf_op jit(solution)/shard_map/psum | solution.py:29
  239.6 7.2 %multiply_reduce_fusion = f32[2048]{0:T(1024)S(1)} fusion(f32[2048]{0:T(1024)S(1)} %broadcast_divide_fusion, f32[2048]{0:T(1024)S(1)} %psum.53, f32[2048,2048]{0,1:T(8,128)} %get-tuple-element.6, f32[2048]{0:T(1024)S(1)} %broadcast_divide_fusion.1), kind=kLoop, calls=%fused_computation.2 | loop fusion | flops 16775168 | bytes 16809984 | tf_op jit(solution)/shard_map/reduce_sum | solution.py:32
  246.8 5.0 %psum.55 = f32[2048]{0:T(1024)S(1)} all-reduce(f32[2048]{0:T(1024)S(1)} %multiply_reduce_fusion), channel_id=1, replica_groups=mesh['rows'=16,'cent'=2] {'cent'}, use_global_device_ids=true, to_apply=%region_15.0 | all-reduce | flops 2048 | bytes 16384 | tf_op jit(solution)/shard_map/psum | solution.py:32
  251.8 15.7 %fusion.3 = f32[1024,2048]{0,1:T(8,128)} fusion(bf16[2048,1024]{1,0:T(8,128)(2,1)} %param.2, f32[2048]{0:T(1024)S(1)} %psum.55, f32[2048]{0:T(1024)S(1)} %broadcast_divide_fusion, f32[2048,2048]{0,1:T(8,128)} %get-tuple-element.6, f32[2048]{0:T(1024)S(1)} %psum.53, f32[2048]{0:T(1024)S(1)} %broadcast_divide_fusion.1), kind=kOutput, calls=%fused_computation.11 | convolution fusion | flops 8610906112 | bytes 29392896 | tf_op jit(solution)/shard_map/dot_general | solution.py:38
  267.5 9.1 %copy.6 = f32[1024,2048]{1,0:T(8,128)} copy(f32[1024,2048]{0,1:T(8,128)} %fusion.3) | data formatting | bytes 16777216
  276.6 0.0 reduce-scatter.4.cloned.1.call-update
  276.6 100.9 %reduce-scatter.4.cloned.1.call-done = f32[64,2048]{1,0:T(8,128)} async-done(((f32[1024,2048]{1,0:T(8,128)}), f32[64,2048]{1,0:T(8,128)}) %reduce-scatter.4.cloned.1.call-update) | async-done | bytes 524304 | tf_op jit(solution)/shard_map/reduce_scatter | solution.py:37
  377.5 1.9 broadcast_multiply_fusion
  (3 shorter events, 0.0 us)
Async XLA Ops:
  6.5 56.1 %all-gather.2.cloned.1.call-start = ((), (), s32[]{:S(2)}) async-start(), calls=%async_computation.1 | async-start | bytes 4456448 | tf_op jit(solution)/shard_map/all_gather | solution.py:18
  7.3 370.3 %reduce-scatter.4.cloned.1.call-start = ((), (), s32[]{:S(2)}) async-start(), calls=%async_computation.2 | async-start | bytes 8912896 | tf_op jit(solution)/shard_map/reduce_scatter | solution.py:37
Sparse Core Ops, SparseCore 0:
  9.5 53.0 all-gather.1
  276.7 100.7 reduce-scatter.3
where the time goes:
time: 387 us; the launch traced here: 386 us
  waiting for transfers between devices  157 us (41%)
  blocking collectives  115 us (30%)
  other arithmetic  60.6 us (16%)
  matrix products  30.9 us (8%)
  between operations  13.5 us (3%)
  local copies, waits for them, and re-layouts  9.11 us (2%)
    reduce_scatter x1, waiting for transfers between devices, on_device(): lax.psum_scatter(lax.dot_general(window, weights, (((0,), (0,)), ((), ())...  101 us
    psum x3, blocking collectives, on_device(): column_mass = lax.psum(column_sum, 'rows')  90.2 us
    all_gather x1, waiting for transfers between devices, on_device(): lax.all_gather(centroids, 'rows', axis=0, tiled=True)  55.3 us
    reduce_sum x3, other arithmetic, on_device(): column_sum = jnp.sum(balanced, axis=0)  27.9 us
    reduce_sum x3, other arithmetic, on_device(): row_mass = lax.psum(jnp.sum(balanced, axis=1), 'cent')  22.3 us
    dot_general x1, matrix products, on_device(): lax.dot_general(window, weights, (((0,), (0,)), ((), ())), preferred_elem...  15.7 us
    dot_general x1, matrix products, on_device(): jnp.dot(window, lax.all_gather(centroids, 'rows', axis=0, tiled=True), pr...  15.2 us
    psum x3, blocking collectives, on_device(): row_mass = lax.psum(jnp.sum(balanced, axis=1), 'cent')  15 us
  transfers between devices with their start and end apart: 2, of which 2 were waited for; matrix products, arithmetic and copies ran while one was open for 0% of the time, Pallas kernels for 0%

commit v1 on v0

--- a/solution.py
+++ b/solution.py
@@ -26,7 +26,11 @@
     target = row_count * lax.axis_size("rows") / K
     for iteration in range(ITERS):
         column_sum = jnp.sum(balanced, axis=0)
-        column_mass = lax.psum(column_sum, "rows")
+        column_mass = column_sum
+        for hop in (1, 2, 4, 8):
+            column_mass = column_mass + lax.ppermute(
+                column_mass, "rows", [(dev, dev ^ hop) for dev in range(16)]
+            )
         column_scale = target / column_mass
         balanced = balanced * column_scale[None, :]
         row_mass = lax.psum(jnp.sum(balanced, axis=1), "cent")

time: 387 us -> 337 us (0.87)
  blocking collectives: 115 us -> 25 us
  waiting for transfers between devices: 157 us -> 186 us
  starting transfers between devices: 0.04 us -> 11.9 us
    psum x3 -> x0, blocking collectives: 90.2 us -> none  [on_device(): column_mass = lax.psum(column_sum, 'rows')]
    ppermute x0 -> x12, waiting for transfers between devices: none -> 27.3 us  [on_device(): lax.ppermute(column_mass, 'rows', [(dev, dev ^ hop) for dev in range(16)])]
    ppermute x0 -> x12, starting transfers between devices: none -> 11.9 us  [on_device(): lax.ppermute(column_mass, 'rows', [(dev, dev ^ hop) for dev in range(16)])]
  transfers between devices with their start and end apart: 2 -> 14, of which waited for: 2 -> 14; matrix products, arithmetic and copies ran while one was open for 0% -> 0% of each run, Pallas kernels for 0% -> 0%
where the time goes in v1:
time: 337 us
  waiting for transfers between devices  186 us (55%)
  other arithmetic  60.6 us (18%)
  matrix products  30.9 us (9%)
  blocking collectives  25 us (7%)
  between operations  13.5 us (4%)
  starting transfers between devices  11.9 us (4%)
  local copies, waits for them, and re-layouts  9.11 us (3%)
    reduce_scatter x1, waiting for transfers between devices, on_device(): lax.psum_scatter(lax.dot_general(window, weights, (((0,), (0,)), ((), ())...  102 us
    all_gather x1, waiting for transfers between devices, on_device(): lax.all_gather(centroids, 'rows', axis=0, tiled=True)  55.3 us
    reduce_sum x3, other arithmetic, on_device(): column_sum = jnp.sum(balanced, axis=0)  27.9 us
    ppermute x12, waiting for transfers between devices, on_device(): lax.ppermute(column_mass, 'rows', [(dev, dev ^ hop) for dev in range(16)])  27.3 us
    reduce_sum x3, other arithmetic, on_device(): row_mass = lax.psum(jnp.sum(balanced, axis=1), 'cent')  22.3 us
    dot_general x1, matrix products, on_device(): lax.dot_general(window, weights, (((0,), (0,)), ((), ())), preferred_elem...  15.7 us
    dot_general x1, matrix products, on_device(): jnp.dot(window, lax.all_gather(centroids, 'rows', axis=0, tiled=True), pr...  15.2 us
    psum x3, blocking collectives, on_device(): row_mass = lax.psum(jnp.sum(balanced, axis=1), 'cent')  15 us
  transfers between devices with their start and end apart: 14, of which 14 were waited for; matrix products, arithmetic and copies ran while one was open for 0% of the time, Pallas kernels for 0%

profile of v1, /device:TPU:0, one launch (start us, length us, event | category | flops | bytes accessed | tf_op | source)
XLA Modules:
  0.0 336.5 jit_solution(1858010201267054964)
XLA Ops:
  6.5 0.0 all-gather.2.cloned.1.call-start
  6.5 0.7 all-gather.2.cloned.1.call-update
  7.3 0.0 reduce-scatter.4.cloned.1.call-start
  7.3 55.3 %all-gather.2.cloned.1.call-done = bf16[1024,2048]{1,0:T(8,128)(2,1)} async-done(((bf16[64,2048]{1,0:T(8,128)(2,1)}), bf16[1024,2048]{1,0:T(8,128)(2,1)}) %all-gather.2.cloned.1.call-update) | async-done | bytes 4194320 | tf_op jit(solution)/shard_map/all_gather | solution.py:18
  62.6 15.2 %multiply_reduce_fusion.3 = (f32[2048]{0:T(1024)S(1)}, f32[2048,2048]{0,1:T(8,128)}) fusion(bf16[2048,1024]{1,0:T(8,128)(2,1)} %param.2, bf16[1024,2048]{1,0:T(8,128)(2,1)} %all-gather.2.cloned.1.call-done), kind=kOutput, calls=%fused_computation.7 | convolution fusion | flops 8598321152 | bytes 25174016 | tf_op jit(solution)/shard_map/dot_general | solution.py:16
  77.9 5.0 %pmax.7 = f32[2048]{0:T(1024)S(1)} all-reduce(f32[2048]{0:T(1024)S(1)} %get-tuple-element.7), channel_id=1, replica_groups=mesh['rows'=16,'cent'=2] {'cent'}, use_global_device_ids=true, to_apply=%region_1.0 | all-reduce | flops 2048 | bytes 16384 | tf_op jit(solution)/shard_map/pmax | solution.py:22
  82.8 8.5 %fusion.1 = f32[2048]{0:T(1024)S(1)} fusion(f32[2048,2048]{0,1:T(8,128)} %get-tuple-element.8, f32[2048]{0:T(1024)S(1)} %pmax.7), kind=kLoop, calls=%fused_computation.9 | loop fusion | flops 12580864 | bytes 16793600 | tf_op jit(solution)/shard_map/reduce_sum | solution.py:24
  91.4 5.0 %psum.28 = f32[2048]{0:T(1024)S(1)} all-reduce(f32[2048]{0:T(1024)S(1)} %fusion.1), channel_id=1, replica_groups=mesh['rows'=16,'cent'=2] {'cent'}, use_global_device_ids=true, to_apply=%region_3.0 | all-reduce | flops 2048 | bytes 16384 | tf_op jit(solution)/shard_map/psum | solution.py:24
  96.4 7.7 %fusion.4 = f32[2048]{0:T(1024)S(1)} fusion(f32[2048]{0:T(1024)S(1)} %psum.28, f32[2048]{0:T(1024)S(1)} %pmax.7, f32[2048,2048]{0,1:T(8,128)} %get-tuple-element.8), kind=kLoop, calls=%fused_computation.16 | loop fusion | flops 16775168 | bytes 16801792 | tf_op jit(solution)/shard_map/reduce_sum | solution.py:28
  104.1 0.1 collective-permute-start
  104.2 1.2 collective-permute-done
  105.3 0.6 collective-permute-start.1
  105.9 3.1 collective-permute-done.1
  109.0 1.5 collective-permute-start.2
  110.5 2.1 collective-permute-done.2
  112.6 1.8 collective-permute-start.3
  114.5 2.7 collective-permute-done.3
  117.2 8.1 %multiply_reduce_fusion.2 = f32[2048]{0:T(1024)S(1)} fusion(f32[2048]{0:T(1024)S(1)} %add_divide_fusion.2, f32[2048]{0:T(1024)S(1)} %psum.28, f32[2048]{0:T(1024)S(1)} %pmax.7, f32[2048,2048]{0,1:T(8,128)} %get-tuple-element.8), kind=kLoop, calls=%fused_computation.6 | loop fusion | flops 20969472 | bytes 16809984 | tf_op jit(solution)/shard_map/reduce_sum | solution.py:36
  125.3 5.0 %psum.29 = f32[2048]{0:T(1024)S(1)} all-reduce(f32[2048]{0:T(1024)S(1)} %multiply_reduce_fusion.2), channel_id=1, replica_groups=mesh['rows'=16,'cent'=2] {'cent'}, use_global_device_ids=true, to_apply=%region_6.0 | all-reduce | flops 2048 | bytes 16384 | tf_op jit(solution)/shard_map/psum | solution.py:36
  130.3 13.1 %fusion.6 = (f32[2048]{0:T(1024)S(1)}, f32[2048,2048]{0,1:T(8,128)}) fusion(f32[2048]{0:T(1024)S(1)} %psum.29, f32[2048]{0:T(1024)S(1)} %add_divide_fusion.2, f32[2048]{0:T(1024)S(1)} %psum.28, f32[2048]{0:T(1024)S(1)} %pmax.7, f32[2048,2048]{0,1:T(8,128)} %get-tuple-element.8), kind=kLoop, calls=%fused_computation.18 | loop fusion | flops 25163776 | bytes 33595392 | tf_op jit(solution)/shard_map/reduce_sum | solution.py:28
  143.4 0.0 collective-permute-start.4
  143.4 1.2 collective-permute-done.4
  144.6 0.6 collective-permute-start.5
  145.1 3.1 collective-permute-done.5
  148.2 1.5 collective-permute-start.6
  149.8 2.1 collective-permute-done.6
  151.9 1.8 collective-permute-start.7
  153.7 2.7 collective-permute-done.7
  156.5 6.9 %multiply_reduce_fusion.1 = f32[2048]{0:T(1024)S(1)} fusion(f32[2048,2048]{0,1:T(8,128)} %get-tuple-element.6, f32[2048]{0:T(1024)S(1)} %add_divide_fusion.1), kind=kLoop, calls=%fused_computation.4 | loop fusion | flops 8386560 | bytes 16793600 | tf_op jit(solution)/shard_map/reduce_sum | solution.py:36
  163.4 5.0 %psum.30 = f32[2048]{0:T(1024)S(1)} all-reduce(f32[2048]{0:T(1024)S(1)} %multiply_reduce_fusion.1), channel_id=1, replica_groups=mesh['rows'=16,'cent'=2] {'cent'}, use_global_device_ids=true, to_apply=%region_9.0 | all-reduce | flops 2048 | bytes 16384 | tf_op jit(solution)/shard_map/psum | solution.py:36
  168.4 7.1 %fusion.5 = f32[2048]{0:T(1024)S(1)} fusion(f32[2048]{0:T(1024)S(1)} %psum.30, f32[2048,2048]{0,1:T(8,128)} %get-tuple-element.6, f32[2048]{0:T(1024)S(1)} %add_divide_fusion.1), kind=kLoop, calls=%fused_computation.17 | loop fusion | flops 12580864 | bytes 16801792 | tf_op jit(solution)/shard_map/reduce_sum | solution.py:28
  175.5 0.1 collective-permute-start.8
  175.6 1.2 collective-permute-done.8
  176.8 0.6 collective-permute-start.9
  177.3 3.1 collective-permute-done.9
  180.4 1.5 collective-permute-start.10
  182.0 2.1 collective-permute-done.10
  184.1 1.8 collective-permute-start.11
  185.9 2.7 collective-permute-done.11
  188.6 7.2 %multiply_reduce_fusion = f32[2048]{0:T(1024)S(1)} fusion(f32[2048]{0:T(1024)S(1)} %add_divide_fusion, f32[2048]{0:T(1024)S(1)} %psum.30, f32[2048,2048]{0,1:T(8,128)} %get-tuple-element.6, f32[2048]{0:T(1024)S(1)} %add_divide_fusion.1), kind=kLoop, calls=%fused_computation.2 | loop fusion | flops 16775168 | bytes 16809984 | tf_op jit(solution)/shard_map/reduce_sum | solution.py:36
  195.9 5.0 %psum.31 = f32[2048]{0:T(1024)S(1)} all-reduce(f32[2048]{0:T(1024)S(1)} %multiply_reduce_fusion), channel_id=1, replica_groups=mesh['rows'=16,'cent'=2] {'cent'}, use_global_device_ids=true, to_apply=%region_12.0 | all-reduce | flops 2048 | bytes 16384 | tf_op jit(solution)/shard_map/psum | solution.py:36
  200.9 15.7 %fusion.3 = f32[1024,2048]{0,1:T(8,128)} fusion(bf16[2048,1024]{1,0:T(8,128)(2,1)} %param.2, f32[2048]{0:T(1024)S(1)} %psum.31, f32[2048]{0:T(1024)S(1)} %add_divide_fusion, f32[2048,2048]{0,1:T(8,128)} %get-tuple-element.6, f32[2048]{0:T(1024)S(1)} %psum.30, f32[2048]{0:T(1024)S(1)} %add_divide_fusion.1), kind=kOutput, calls=%fused_computation.11 | convolution fusion | flops 8610906112 | bytes 29392896 | tf_op jit(solution)/shard_map/dot_general | solution.py:42
  216.5 9.1 %copy.6 = f32[1024,2048]{1,0:T(8,128)} copy(f32[1024,2048]{0,1:T(8,128)} %fusion.3) | data formatting | bytes 16777216
  225.6 0.0 reduce-scatter.4.cloned.1.call-update
  225.7 102.2 %reduce-scatter.4.cloned.1.call-done = f32[64,2048]{1,0:T(8,128)} async-done(((f32[1024,2048]{1,0:T(8,128)}), f32[64,2048]{1,0:T(8,128)}) %reduce-scatter.4.cloned.1.call-update) | async-done | bytes 524304 | tf_op jit(solution)/shard_map/reduce_scatter | solution.py:41
  327.8 1.9 broadcast_multiply_fusion
  (12 shorter events, 0.0 us)
Async XLA Ops:
  6.5 56.1 %all-gather.2.cloned.1.call-start = ((), (), s32[]{:S(2)}) async-start(), calls=%async_computation.1 | async-start | bytes 4456448 | tf_op jit(solution)/shard_map/all_gather | solution.py:18
  7.3 320.6 %reduce-scatter.4.cloned.1.call-start = ((), (), s32[]{:S(2)}) async-start(), calls=%async_computation.2 | async-start | bytes 8912896 | tf_op jit(solution)/shard_map/reduce_scatter | solution.py:41
  104.1 1.2 collective-permute-start
  105.3 3.7 %collective-permute-start.1 = (f32[2048]{0:T(1024)S(1)}, f32[2048]{0:T(1024)S(1)}, u32[]{:S(2)}, u32[]{:S(2)}) collective-permute-start(f32[2048]{0:T(1024)S(1)} %add.46), channel_id=1, source_target_pairs={{0,4},{2,6},{4,0},{6,2},{8,12},{10,14},{12,8},{14,10},{16,20},{18,... | collective-permute-start | bytes 24584 | tf_op jit(solution)/shard_map/ppermute | solution.py:31
  109.0 3.7 %collective-permute-start.2 = (f32[2048]{0:T(1024)S(1)}, f32[2048]{0:T(1024)S(1)}, u32[]{:S(2)}, u32[]{:S(2)}) collective-permute-start(f32[2048]{0:T(1024)S(1)} %add.47), channel_id=1, source_target_pairs={{0,8},{2,10},{4,12},{6,14},{8,0},{10,2},{12,4},{14,6},{16,24},{18,... | collective-permute-start | bytes 24584 | tf_op jit(solution)/shard_map/ppermute | solution.py:31
  112.6 4.5 %collective-permute-start.3 = (f32[2048]{0:T(1024)S(1)}, f32[2048]{0:T(1024)S(1)}, u32[]{:S(2)}, u32[]{:S(2)}) collective-permute-start(f32[2048]{0:T(1024)S(1)} %add.48), channel_id=1, source_target_pairs={{0,16},{2,18},{4,20},{6,22},{8,24},{10,26},{12,28},{14,30},{16,0},... | collective-permute-start | bytes 24584 | tf_op jit(solution)/shard_map/ppermute | solution.py:31
  143.4 1.2 collective-permute-start.4
  144.6 3.7 %collective-permute-start.5 = (f32[2048]{0:T(1024)S(1)}, f32[2048]{0:T(1024)S(1)}, u32[]{:S(2)}, u32[]{:S(2)}) collective-permute-start(f32[2048]{0:T(1024)S(1)} %add.50), channel_id=1, source_target_pairs={{0,4},{2,6},{4,0},{6,2},{8,12},{10,14},{12,8},{14,10},{16,20},{18,... | collective-permute-start | bytes 24584 | tf_op jit(solution)/shard_map/ppermute | solution.py:31
  148.2 3.7 %collective-permute-start.6 = (f32[2048]{0:T(1024)S(1)}, f32[2048]{0:T(1024)S(1)}, u32[]{:S(2)}, u32[]{:S(2)}) collective-permute-start(f32[2048]{0:T(1024)S(1)} %add.51), channel_id=1, source_target_pairs={{0,8},{2,10},{4,12},{6,14},{8,0},{10,2},{12,4},{14,6},{16,24},{18,... | collective-permute-start | bytes 24584 | tf_op jit(solution)/shard_map/ppermute | solution.py:31
  151.9 4.5 %collective-permute-start.7 = (f32[2048]{0:T(1024)S(1)}, f32[2048]{0:T(1024)S(1)}, u32[]{:S(2)}, u32[]{:S(2)}) collective-permute-start(f32[2048]{0:T(1024)S(1)} %add.52), channel_id=1, source_target_pairs={{0,16},{2,18},{4,20},{6,22},{8,24},{10,26},{12,28},{14,30},{16,0},... | collective-permute-start | bytes 24584 | tf_op jit(solution)/shard_map/ppermute | solution.py:31
  175.5 1.2 collective-permute-start.8
  176.8 3.7 %collective-permute-start.9 = (f32[2048]{0:T(1024)S(1)}, f32[2048]{0:T(1024)S(1)}, u32[]{:S(2)}, u32[]{:S(2)}) collective-permute-start(f32[2048]{0:T(1024)S(1)} %add.54), channel_id=1, source_target_pairs={{0,4},{2,6},{4,0},{6,2},{8,12},{10,14},{12,8},{14,10},{16,20},{18,... | collective-permute-start | bytes 24584 | tf_op jit(solution)/shard_map/ppermute | solution.py:31
  180.4 3.7 %collective-permute-start.10 = (f32[2048]{0:T(1024)S(1)}, f32[2048]{0:T(1024)S(1)}, u32[]{:S(2)}, u32[]{:S(2)}) collective-permute-start(f32[2048]{0:T(1024)S(1)} %add.55), channel_id=1, source_target_pairs={{0,8},{2,10},{4,12},{6,14},{8,0},{10,2},{12,4},{14,6},{16,24},{18,... | collective-permute-start | bytes 24584 | tf_op jit(solution)/shard_map/ppermute | solution.py:31
  184.1 4.5 %collective-permute-start.11 = (f32[2048]{0:T(1024)S(1)}, f32[2048]{0:T(1024)S(1)}, u32[]{:S(2)}, u32[]{:S(2)}) collective-permute-start(f32[2048]{0:T(1024)S(1)} %add.56), channel_id=1, source_target_pairs={{0,16},{2,18},{4,20},{6,22},{8,24},{10,26},{12,28},{14,30},{16,0},... | collective-permute-start | bytes 24584 | tf_op jit(solution)/shard_map/ppermute | solution.py:31
Sparse Core Ops, SparseCore 0:
  9.5 53.0 all-gather.1
  225.8 102.0 reduce-scatter.3
